TPU v7x, 256 devices: a whole 4x4x8 slice. The times are simulated.
256 devices in a mesh: blk: 32 (over y_hi, z, core), lag: 8 (over y_lo, x).
Axes of the slice: x: 4, y: 4 (y_hi: 2, y_lo: 2; y = y_hi * 2 + y_lo), z: 8, core: 2. Of those that a mesh axis runs over, the one named last changes fastest.
Arguments:
- spectra: bfloat16 [4096, 3, 2, 1024], P('blk', None, None, 'lag'), may hold values from -6 to 6
- band: int32 [4096, 2], P('blk'), may hold values from 0 to 1024, as said below
- pair_lists: int32 [32, 17, 96, 2], P('blk'), may hold values from 0 to 127
- pair_counts: int32 [32, 17], P('blk'), may hold values from 32 to 96, as said below
Outputs:
- gradient: float32 [4096, 3, 2, 1024], P('blk', None, None, 'lag')
Inputs may be any that keep to these rules, and one draw needn't show every extreme that they name: band[s, 0] < band[s, 1]; band[s, 0] is at most 128 and band[s, 1] at least 896; some station starts at 0 and some ends at 1024. `pair_counts`: at least a third of the slots are used; in every block one offset uses all 96 slots.
All inputs are finite; a program needn't handle non-finite values.
Results may differ from a plain program's by a relative error of at most 0.0045.
Values may be sent and summed in bfloat16 or wider, within the bound.
No kernel may reach another device: no remote copies, remote signals or barrier semaphores. Data moves between devices by JAX's collectives and lax.ppermute only.
A program may use at most 64 MiB of HBM per device.

v0:
```python
import math
import jax
import jax.numpy as jnp
from jax import lax
from jax.sharding import PartitionSpec as P


def from_behind(block, axis, distance):
    devices = range(lax.axis_size(axis))
    route = [((i - distance) % len(devices), i) for i in devices]
    return lax.ppermute(block, axis, route)


def phase_table(freq_ids, lag_ids, lag_total, freq_total):
    turns = freq_ids[:, None] * lag_ids[None, :] % lag_total
    angle = turns.astype(jnp.float32) * (2.0 * jnp.pi / lag_total)
    factor = 1.0 / jnp.sqrt(jnp.float32(freq_total))
    return jnp.stack([jnp.cos(angle) * factor, -jnp.sin(angle) * factor], 0).astype(jnp.bfloat16)


def whiten(spectra, band, freq_ids):
    values = spectra.astype(jnp.float32)
    meansq = jnp.mean(values * values, axis=(1, 2))
    inside = (freq_ids[None, :] >= band[:, 0:1]) & (freq_ids[None, :] < band[:, 1:2])
    factor = jnp.where(inside, 1.0 / jnp.sqrt(jnp.maximum(meansq, 0.25)), 0.0)
    return (values * factor[:, None, None, :]).astype(jnp.bfloat16)


def on_device(spectra, band, pair_lists, pair_counts):
    stations, comps, parts, bins_local = spectra.shape
    slots = pair_lists.shape[2]
    steps = pair_lists.shape[1]
    lanes = lax.axis_size("lag")
    freq_total = bins_local * lanes
    lag_total = 2 * freq_total
    lag_local = lag_total // lanes
    width = comps * parts * bins_local
    lane = lax.axis_index("lag")
    freq_ids = lane * bins_local + jnp.arange(bins_local, dtype=jnp.int32)
    lag_ids = lane * lag_local + jnp.arange(lag_local, dtype=jnp.int32)
    resident = whiten(spectra, band, freq_ids)
    local_table = phase_table(
        freq_ids, jnp.arange(lag_total, dtype=jnp.int32), lag_total, freq_total
    )
    weight = 1.0 + 3.0 * lag_ids.astype(jnp.float32) / lag_total
    station_ids = jnp.arange(stations, dtype=jnp.int32)
    slot_ids = jnp.arange(slots, dtype=jnp.int32)

    def forward(cross):
        return lax.psum_scatter(
            jnp.einsum("prf,rft->tp", cross, local_table, preferred_element_type=jnp.float32),
            "lag",
            scatter_dimension=0,
            tiled=True,
        ).T

    def back(piece):
        return jnp.einsum("pt,rft->prf", piece, local_table, preferred_element_type=jnp.float32)

    def correlate(arriving, pairs, count):
        first = pairs[:, 0]
        second = pairs[:, 1]
        pick_first = (first[:, None] == station_ids[None, :]).astype(jnp.bfloat16)
        pick_second = (second[:, None] == station_ids[None, :]).astype(jnp.bfloat16)
        rows_a = jnp.dot(
            pick_first, resident.reshape(stations, width), preferred_element_type=jnp.float32
        )
        rows_b = jnp.dot(
            pick_second, arriving.reshape(stations, width), preferred_element_type=jnp.float32
        )
        rows_a = rows_a.reshape(slots, comps, parts, bins_local)
        rows_b = rows_b.reshape(slots, comps, parts, bins_local)
        real_a, imag_a = (rows_a[:, :, 0], rows_a[:, :, 1])
        real_b, imag_b = (rows_b[:, :, 0], rows_b[:, :, 1])
        valid = (slot_ids < count).astype(jnp.float32)[:, None]
        cross_real = jnp.sum(real_a * real_b + imag_a * imag_b, axis=1) * valid
        cross_imag = jnp.sum(imag_a * real_b - real_a * imag_b, axis=1) * valid
        cross = jnp.stack([cross_real, cross_imag], 1).astype(jnp.bfloat16)
        lagged = forward(cross)
        energy = lax.psum(jnp.sum(weight[None, :] * lagged * lagged, axis=1) / lag_total, "lag")
        adjoint = (weight[None, :] * lagged / jnp.sqrt(energy + 1e-05)[:, None]).astype(
            jnp.bfloat16
        )
        spectral = back(lax.all_gather(adjoint, "lag", axis=1, tiled=True))
        adj_real = spectral[:, None, 0]
        adj_imag = spectral[:, None, 1]
        near = jnp.stack(
            [adj_real * real_b - adj_imag * imag_b, adj_real * imag_b + adj_imag * real_b], 2
        )
        far = jnp.stack(
            [adj_real * real_a + adj_imag * imag_a, adj_real * imag_a - adj_imag * real_a], 2
        )
        near = near.astype(jnp.bfloat16).reshape(slots, width)
        far = far.astype(jnp.bfloat16).reshape(slots, width)
        own = jnp.einsum("ps,pw->sw", pick_first, near, preferred_element_type=jnp.float32)
        return (own, far, second, pick_second)

    def visit(step, arriving, total, carried):
        own, far, second, pick_second = correlate(
            arriving, pair_lists[0, step], pair_counts[0, step]
        )
        total = total + own
        carried = carried + jnp.einsum(
            "ps,pw->sw", pick_second, far, preferred_element_type=jnp.float32
        )
        return (total, carried)

    def advance(step, state):
        arriving, total, carried = state
        arriving = from_behind(arriving, "blk", 1)
        carried = from_behind(carried, "blk", 1)
        total, carried = visit(step, arriving, total, carried)
        return (arriving, total, carried)

    start_carried = jnp.zeros((stations, width), jnp.float32)
    total, carried = visit(0, resident, jnp.zeros((stations, width), jnp.float32), start_carried)
    arriving, total, carried = lax.fori_loop(1, steps, advance, (resident, total, carried))
    total = total + from_behind(carried, "blk", -(steps - 1))
    gradient = total / math.sqrt(slots)
    return gradient.reshape(stations, comps, parts, bins_local)


def solution(mesh):
    in_specs = (
        P("blk", None, None, "lag"),
        P("blk", None),
        P("blk", None, None, None),
        P("blk", None),
    )
    out_specs = P("blk", None, None, "lag")
    return jax.shard_map(
        on_device, mesh=mesh, in_specs=in_specs, out_specs=out_specs, check_vma=False
    )
```

profile of v0, /device:TPU:8, one launch (start us, length us, event | category | flops | bytes accessed | tf_op | source)
XLA Modules:
  0.0 1684.5 jit_solution(6176703667037175156)
XLA Ops:
  16.2 42.7 %reduce-scatter.3.cloned.1.call-done = f32[256,96]{0,1:T(8,128)} async-done(((f32[2048,96]{0,1:T(8,128)}), f32[256,96]{0,1:T(8,128)}) %reduce-scatter.3.cloned.1.call-update) | async-done | bytes 98320 | tf_op jit(solution)/shard_map/reduce_scatter | solution.py:50
  60.0 17.5 %psum.21 = f32[96]{0:T(128)S(1)} all-reduce(f32[96]{0:T(128)S(1)} %broadcast_multiply_fusion.1), channel_id=1, replica_groups=mesh['blk'=32,'lag'=8] {'lag'}, use_global_device_ids=true, to_apply=%region_5.6 | all-reduce | flops 96 | bytes 768 | tf_op jit(solution)/shard_map/psum | solution.py:80
  78.5 28.8 %all_gather.13 = bf16[96,2048]{1,0:T(8,128)(2,1)S(1)} all-gather(bf16[96,256]{1,0:T(8,128)(2,1)S(1)} %fusion.43), channel_id=1, replica_groups=mesh['blk'=32,'lag'=8] {'lag'}, dimensions={1}, use_global_device_ids=true | all-gather | bytes 442368 | tf_op jit(solution)/shard_map/all_gather | solution.py:84
  109.0 1558.6 %while.21 = (s32[]{:T(128)}, bf16[128,3,2,128]{0,3,2,1:T(8,128)(2,1)S(1)}, f32[128,768]{1,0:T(8,128)S(1)}, f32[128,768]{1,0:T(8,128)S(1)}, s32[1,17,96,2]{2,3,1,...) while((s32[]{:T(128)}, ...), condition=%wide.region_12.13_spmd.clone.clone, body=%wide.region_6.12_spmd.clone.clone.sunk | while | flops 278300032 | bytes 16166447 | solution.py:117
  119.6 36.8 %reduce-scatter.5.cloned.1.call-done = f32[256,96]{0,1:T(8,128)} async-done(((f32[2048,96]{0,1:T(8,128)}), f32[256,96]{0,1:T(8,128)}) %reduce-scatter.5.cloned.1.call-update) | async-done | bytes 98320 | tf_op jit(solution)/shard_map/while/body/eval_jaxpr/reduce_scatter | solution.py:50
  157.3 17.6 %psum.25 = f32[96]{0:T(128)S(1)} all-reduce(f32[96]{0:T(128)S(1)} %broadcast_multiply_fusion.3), channel_id=1, replica_groups=mesh['blk'=32,'lag'=8] {'lag'}, use_global_device_ids=true, to_apply=%region_11.11 | all-reduce | flops 96 | bytes 768 | tf_op jit(solution)/shard_map/while/body/eval_jaxpr/psum | solution.py:80
  175.9 28.8 %all_gather.17 = bf16[96,2048]{1,0:T(8,128)(2,1)S(1)} all-gather(bf16[96,256]{1,0:T(8,128)(2,1)S(1)} %fusion.96), channel_id=1, replica_groups=mesh['blk'=32,'lag'=8] {'lag'}, dimensions={1}, use_global_device_ids=true | all-gather | bytes 442368 | tf_op jit(solution)/shard_map/while/body/eval_jaxpr/all_gather | solution.py:84
  208.8 6.5 collective-permute-done
  217.0 36.7 %reduce-scatter.5.cloned.1.call-done = f32[256,96]{0,1:T(8,128)} async-done(((f32[2048,96]{0,1:T(8,128)}), f32[256,96]{0,1:T(8,128)}) %reduce-scatter.5.cloned.1.call-update) | async-done | bytes 98320 | tf_op jit(solution)/shard_map/while/body/eval_jaxpr/reduce_scatter | solution.py:50
  254.8 17.4 %psum.25 = f32[96]{0:T(128)S(1)} all-reduce(f32[96]{0:T(128)S(1)} %broadcast_multiply_fusion.3), channel_id=1, replica_groups=mesh['blk'=32,'lag'=8] {'lag'}, use_global_device_ids=true, to_apply=%region_11.11 | all-reduce | flops 96 | bytes 768 | tf_op jit(solution)/shard_map/while/body/eval_jaxpr/psum | solution.py:80
  273.2 28.8 %all_gather.17 = bf16[96,2048]{1,0:T(8,128)(2,1)S(1)} all-gather(bf16[96,256]{1,0:T(8,128)(2,1)S(1)} %fusion.96), channel_id=1, replica_groups=mesh['blk'=32,'lag'=8] {'lag'}, dimensions={1}, use_global_device_ids=true | all-gather | bytes 442368 | tf_op jit(solution)/shard_map/while/body/eval_jaxpr/all_gather | solution.py:84
  306.1 6.5 collective-permute-done
  314.4 36.8 %reduce-scatter.5.cloned.1.call-done = f32[256,96]{0,1:T(8,128)} async-done(((f32[2048,96]{0,1:T(8,128)}), f32[256,96]{0,1:T(8,128)}) %reduce-scatter.5.cloned.1.call-update) | async-done | bytes 98320 | tf_op jit(solution)/shard_map/while/body/eval_jaxpr/reduce_scatter | solution.py:50
  352.2 17.5 %psum.25 = f32[96]{0:T(128)S(1)} all-reduce(f32[96]{0:T(128)S(1)} %broadcast_multiply_fusion.3), channel_id=1, replica_groups=mesh['blk'=32,'lag'=8] {'lag'}, use_global_device_ids=true, to_apply=%region_11.11 | all-reduce | flops 96 | bytes 768 | tf_op jit(solution)/shard_map/while/body/eval_jaxpr/psum | solution.py:80
  370.7 28.9 %all_gather.17 = bf16[96,2048]{1,0:T(8,128)(2,1)S(1)} all-gather(bf16[96,256]{1,0:T(8,128)(2,1)S(1)} %fusion.96), channel_id=1, replica_groups=mesh['blk'=32,'lag'=8] {'lag'}, dimensions={1}, use_global_device_ids=true | all-gather | bytes 442368 | tf_op jit(solution)/shard_map/while/body/eval_jaxpr/all_gather | solution.py:84
  403.7 6.5 collective-permute-done
  411.9 36.6 %reduce-scatter.5.cloned.1.call-done = f32[256,96]{0,1:T(8,128)} async-done(((f32[2048,96]{0,1:T(8,128)}), f32[256,96]{0,1:T(8,128)}) %reduce-scatter.5.cloned.1.call-update) | async-done | bytes 98320 | tf_op jit(solution)/shard_map/while/body/eval_jaxpr/reduce_scatter | solution.py:50
  449.6 17.5 %psum.25 = f32[96]{0:T(128)S(1)} all-reduce(f32[96]{0:T(128)S(1)} %broadcast_multiply_fusion.3), channel_id=1, replica_groups=mesh['blk'=32,'lag'=8] {'lag'}, use_global_device_ids=true, to_apply=%region_11.11 | all-reduce | flops 96 | bytes 768 | tf_op jit(solution)/shard_map/while/body/eval_jaxpr/psum | solution.py:80
  468.1 28.8 %all_gather.17 = bf16[96,2048]{1,0:T(8,128)(2,1)S(1)} all-gather(bf16[96,256]{1,0:T(8,128)(2,1)S(1)} %fusion.96), channel_id=1, replica_groups=mesh['blk'=32,'lag'=8] {'lag'}, dimensions={1}, use_global_device_ids=true | all-gather | bytes 442368 | tf_op jit(solution)/shard_map/while/body/eval_jaxpr/all_gather | solution.py:84
  501.0 6.5 collective-permute-done
  509.2 36.8 %reduce-scatter.5.cloned.1.call-done = f32[256,96]{0,1:T(8,128)} async-done(((f32[2048,96]{0,1:T(8,128)}), f32[256,96]{0,1:T(8,128)}) %reduce-scatter.5.cloned.1.call-update) | async-done | bytes 98320 | tf_op jit(solution)/shard_map/while/body/eval_jaxpr/reduce_scatter | solution.py:50
  547.0 17.4 %psum.25 = f32[96]{0:T(128)S(1)} all-reduce(f32[96]{0:T(128)S(1)} %broadcast_multiply_fusion.3), channel_id=1, replica_groups=mesh['blk'=32,'lag'=8] {'lag'}, use_global_device_ids=true, to_apply=%region_11.11 | all-reduce | flops 96 | bytes 768 | tf_op jit(solution)/shard_map/while/body/eval_jaxpr/psum | solution.py:80
  565.5 28.8 %all_gather.17 = bf16[96,2048]{1,0:T(8,128)(2,1)S(1)} all-gather(bf16[96,256]{1,0:T(8,128)(2,1)S(1)} %fusion.96), channel_id=1, replica_groups=mesh['blk'=32,'lag'=8] {'lag'}, dimensions={1}, use_global_device_ids=true | all-gather | bytes 442368 | tf_op jit(solution)/shard_map/while/body/eval_jaxpr/all_gather | solution.py:84
  598.4 6.5 collective-permute-done
  606.6 36.8 %reduce-scatter.5.cloned.1.call-done = f32[256,96]{0,1:T(8,128)} async-done(((f32[2048,96]{0,1:T(8,128)}), f32[256,96]{0,1:T(8,128)}) %reduce-scatter.5.cloned.1.call-update) | async-done | bytes 98320 | tf_op jit(solution)/shard_map/while/body/eval_jaxpr/reduce_scatter | solution.py:50
  644.4 17.5 %psum.25 = f32[96]{0:T(128)S(1)} all-reduce(f32[96]{0:T(128)S(1)} %broadcast_multiply_fusion.3), channel_id=1, replica_groups=mesh['blk'=32,'lag'=8] {'lag'}, use_global_device_ids=true, to_apply=%region_11.11 | all-reduce | flops 96 | bytes 768 | tf_op jit(solution)/shard_map/while/body/eval_jaxpr/psum | solution.py:80
  662.9 28.9 %all_gather.17 = bf16[96,2048]{1,0:T(8,128)(2,1)S(1)} all-gather(bf16[96,256]{1,0:T(8,128)(2,1)S(1)} %fusion.96), channel_id=1, replica_groups=mesh['blk'=32,'lag'=8] {'lag'}, dimensions={1}, use_global_device_ids=true | all-gather | bytes 442368 | tf_op jit(solution)/shard_map/while/body/eval_jaxpr/all_gather | solution.py:84
  704.1 36.7 %reduce-scatter.5.cloned.1.call-done = f32[256,96]{0,1:T(8,128)} async-done(((f32[2048,96]{0,1:T(8,128)}), f32[256,96]{0,1:T(8,128)}) %reduce-scatter.5.cloned.1.call-update) | async-done | bytes 98320 | tf_op jit(solution)/shard_map/while/body/eval_jaxpr/reduce_scatter | solution.py:50
  741.8 17.5 %psum.25 = f32[96]{0:T(128)S(1)} all-reduce(f32[96]{0:T(128)S(1)} %broadcast_multiply_fusion.3), channel_id=1, replica_groups=mesh['blk'=32,'lag'=8] {'lag'}, use_global_device_ids=true, to_apply=%region_11.11 | all-reduce | flops 96 | bytes 768 | tf_op jit(solution)/shard_map/while/body/eval_jaxpr/psum | solution.py:80
  760.3 28.9 %all_gather.17 = bf16[96,2048]{1,0:T(8,128)(2,1)S(1)} all-gather(bf16[96,256]{1,0:T(8,128)(2,1)S(1)} %fusion.96), channel_id=1, replica_groups=mesh['blk'=32,'lag'=8] {'lag'}, dimensions={1}, use_global_device_ids=true | all-gather | bytes 442368 | tf_op jit(solution)/shard_map/while/body/eval_jaxpr/all_gather | solution.py:84
  793.2 6.5 collective-permute-done
  801.5 36.8 %reduce-scatter.5.cloned.1.call-done = f32[256,96]{0,1:T(8,128)} async-done(((f32[2048,96]{0,1:T(8,128)}), f32[256,96]{0,1:T(8,128)}) %reduce-scatter.5.cloned.1.call-update) | async-done | bytes 98320 | tf_op jit(solution)/shard_map/while/body/eval_jaxpr/reduce_scatter | solution.py:50
  839.3 17.5 %psum.25 = f32[96]{0:T(128)S(1)} all-reduce(f32[96]{0:T(128)S(1)} %broadcast_multiply_fusion.3), channel_id=1, replica_groups=mesh['blk'=32,'lag'=8] {'lag'}, use_global_device_ids=true, to_apply=%region_11.11 | all-reduce | flops 96 | bytes 768 | tf_op jit(solution)/shard_map/while/body/eval_jaxpr/psum | solution.py:80
  857.7 28.9 %all_gather.17 = bf16[96,2048]{1,0:T(8,128)(2,1)S(1)} all-gather(bf16[96,256]{1,0:T(8,128)(2,1)S(1)} %fusion.96), channel_id=1, replica_groups=mesh['blk'=32,'lag'=8] {'lag'}, dimensions={1}, use_global_device_ids=true | all-gather | bytes 442368 | tf_op jit(solution)/shard_map/while/body/eval_jaxpr/all_gather | solution.py:84
  890.7 6.5 collective-permute-done
  898.9 36.7 %reduce-scatter.5.cloned.1.call-done = f32[256,96]{0,1:T(8,128)} async-done(((f32[2048,96]{0,1:T(8,128)}), f32[256,96]{0,1:T(8,128)}) %reduce-scatter.5.cloned.1.call-update) | async-done | bytes 98320 | tf_op jit(solution)/shard_map/while/body/eval_jaxpr/reduce_scatter | solution.py:50
  936.6 17.5 %psum.25 = f32[96]{0:T(128)S(1)} all-reduce(f32[96]{0:T(128)S(1)} %broadcast_multiply_fusion.3), channel_id=1, replica_groups=mesh['blk'=32,'lag'=8] {'lag'}, use_global_device_ids=true, to_apply=%region_11.11 | all-reduce | flops 96 | bytes 768 | tf_op jit(solution)/shard_map/while/body/eval_jaxpr/psum | solution.py:80
  955.2 28.8 %all_gather.17 = bf16[96,2048]{1,0:T(8,128)(2,1)S(1)} all-gather(bf16[96,256]{1,0:T(8,128)(2,1)S(1)} %fusion.96), channel_id=1, replica_groups=mesh['blk'=32,'lag'=8] {'lag'}, dimensions={1}, use_global_device_ids=true | all-gather | bytes 442368 | tf_op jit(solution)/shard_map/while/body/eval_jaxpr/all_gather | solution.py:84
  988.0 6.5 collective-permute-done
  996.3 36.7 %reduce-scatter.5.cloned.1.call-done = f32[256,96]{0,1:T(8,128)} async-done(((f32[2048,96]{0,1:T(8,128)}), f32[256,96]{0,1:T(8,128)}) %reduce-scatter.5.cloned.1.call-update) | async-done | bytes 98320 | tf_op jit(solution)/shard_map/while/body/eval_jaxpr/reduce_scatter | solution.py:50
  1034.0 17.6 %psum.25 = f32[96]{0:T(128)S(1)} all-reduce(f32[96]{0:T(128)S(1)} %broadcast_multiply_fusion.3), channel_id=1, replica_groups=mesh['blk'=32,'lag'=8] {'lag'}, use_global_device_ids=true, to_apply=%region_11.11 | all-reduce | flops 96 | bytes 768 | tf_op jit(solution)/shard_map/while/body/eval_jaxpr/psum | solution.py:80
  1052.6 28.8 %all_gather.17 = bf16[96,2048]{1,0:T(8,128)(2,1)S(1)} all-gather(bf16[96,256]{1,0:T(8,128)(2,1)S(1)} %fusion.96), channel_id=1, replica_groups=mesh['blk'=32,'lag'=8] {'lag'}, dimensions={1}, use_global_device_ids=true | all-gather | bytes 442368 | tf_op jit(solution)/shard_map/while/body/eval_jaxpr/all_gather | solution.py:84
  1093.6 36.8 %reduce-scatter.5.cloned.1.call-done = f32[256,96]{0,1:T(8,128)} async-done(((f32[2048,96]{0,1:T(8,128)}), f32[256,96]{0,1:T(8,128)}) %reduce-scatter.5.cloned.1.call-update) | async-done | bytes 98320 | tf_op jit(solution)/shard_map/while/body/eval_jaxpr/reduce_scatter | solution.py:50
  1131.4 17.5 %psum.25 = f32[96]{0:T(128)S(1)} all-reduce(f32[96]{0:T(128)S(1)} %broadcast_multiply_fusion.3), channel_id=1, replica_groups=mesh['blk'=32,'lag'=8] {'lag'}, use_global_device_ids=true, to_apply=%region_11.11 | all-reduce | flops 96 | bytes 768 | tf_op jit(solution)/shard_map/while/body/eval_jaxpr/psum | solution.py:80
  1149.9 28.9 %all_gather.17 = bf16[96,2048]{1,0:T(8,128)(2,1)S(1)} all-gather(bf16[96,256]{1,0:T(8,128)(2,1)S(1)} %fusion.96), channel_id=1, replica_groups=mesh['blk'=32,'lag'=8] {'lag'}, dimensions={1}, use_global_device_ids=true | all-gather | bytes 442368 | tf_op jit(solution)/shard_map/while/body/eval_jaxpr/all_gather | solution.py:84
  1182.9 6.5 collective-permute-done
  1191.1 36.7 %reduce-scatter.5.cloned.1.call-done = f32[256,96]{0,1:T(8,128)} async-done(((f32[2048,96]{0,1:T(8,128)}), f32[256,96]{0,1:T(8,128)}) %reduce-scatter.5.cloned.1.call-update) | async-done | bytes 98320 | tf_op jit(solution)/shard_map/while/body/eval_jaxpr/reduce_scatter | solution.py:50
  1228.8 17.5 %psum.25 = f32[96]{0:T(128)S(1)} all-reduce(f32[96]{0:T(128)S(1)} %broadcast_multiply_fusion.3), channel_id=1, replica_groups=mesh['blk'=32,'lag'=8] {'lag'}, use_global_device_ids=true, to_apply=%region_11.11 | all-reduce | flops 96 | bytes 768 | tf_op jit(solution)/shard_map/while/body/eval_jaxpr/psum | solution.py:80
  1247.3 28.8 %all_gather.17 = bf16[96,2048]{1,0:T(8,128)(2,1)S(1)} all-gather(bf16[96,256]{1,0:T(8,128)(2,1)S(1)} %fusion.96), channel_id=1, replica_groups=mesh['blk'=32,'lag'=8] {'lag'}, dimensions={1}, use_global_device_ids=true | all-gather | bytes 442368 | tf_op jit(solution)/shard_map/while/body/eval_jaxpr/all_gather | solution.py:84
  1280.2 6.5 collective-permute-done
  1288.5 36.8 %reduce-scatter.5.cloned.1.call-done = f32[256,96]{0,1:T(8,128)} async-done(((f32[2048,96]{0,1:T(8,128)}), f32[256,96]{0,1:T(8,128)}) %reduce-scatter.5.cloned.1.call-update) | async-done | bytes 98320 | tf_op jit(solution)/shard_map/while/body/eval_jaxpr/reduce_scatter | solution.py:50
  1326.2 17.5 %psum.25 = f32[96]{0:T(128)S(1)} all-reduce(f32[96]{0:T(128)S(1)} %broadcast_multiply_fusion.3), channel_id=1, replica_groups=mesh['blk'=32,'lag'=8] {'lag'}, use_global_device_ids=true, to_apply=%region_11.11 | all-reduce | flops 96 | bytes 768 | tf_op jit(solution)/shard_map/while/body/eval_jaxpr/psum | solution.py:80
  1344.7 28.9 %all_gather.17 = bf16[96,2048]{1,0:T(8,128)(2,1)S(1)} all-gather(bf16[96,256]{1,0:T(8,128)(2,1)S(1)} %fusion.96), channel_id=1, replica_groups=mesh['blk'=32,'lag'=8] {'lag'}, dimensions={1}, use_global_device_ids=true | all-gather | bytes 442368 | tf_op jit(solution)/shard_map/while/body/eval_jaxpr/all_gather | solution.py:84
  1377.7 6.5 collective-permute-done
  1385.9 36.7 %reduce-scatter.5.cloned.1.call-done = f32[256,96]{0,1:T(8,128)} async-done(((f32[2048,96]{0,1:T(8,128)}), f32[256,96]{0,1:T(8,128)}) %reduce-scatter.5.cloned.1.call-update) | async-done | bytes 98320 | tf_op jit(solution)/shard_map/while/body/eval_jaxpr/reduce_scatter | solution.py:50
  1423.6 17.5 %psum.25 = f32[96]{0:T(128)S(1)} all-reduce(f32[96]{0:T(128)S(1)} %broadcast_multiply_fusion.3), channel_id=1, replica_groups=mesh['blk'=32,'lag'=8] {'lag'}, use_global_device_ids=true, to_apply=%region_11.11 | all-reduce | flops 96 | bytes 768 | tf_op jit(solution)/shard_map/while/body/eval_jaxpr/psum | solution.py:80
  1442.1 28.9 %all_gather.17 = bf16[96,2048]{1,0:T(8,128)(2,1)S(1)} all-gather(bf16[96,256]{1,0:T(8,128)(2,1)S(1)} %fusion.96), channel_id=1, replica_groups=mesh['blk'=32,'lag'=8] {'lag'}, dimensions={1}, use_global_device_ids=true | all-gather | bytes 442368 | tf_op jit(solution)/shard_map/while/body/eval_jaxpr/all_gather | solution.py:84
  1483.3 36.7 %reduce-scatter.5.cloned.1.call-done = f32[256,96]{0,1:T(8,128)} async-done(((f32[2048,96]{0,1:T(8,128)}), f32[256,96]{0,1:T(8,128)}) %reduce-scatter.5.cloned.1.call-update) | async-done | bytes 98320 | tf_op jit(solution)/shard_map/while/body/eval_jaxpr/reduce_scatter | solution.py:50
  1521.0 17.5 %psum.25 = f32[96]{0:T(128)S(1)} all-reduce(f32[96]{0:T(128)S(1)} %broadcast_multiply_fusion.3), channel_id=1, replica_groups=mesh['blk'=32,'lag'=8] {'lag'}, use_global_device_ids=true, to_apply=%region_11.11 | all-reduce | flops 96 | bytes 768 | tf_op jit(solution)/shard_map/while/body/eval_jaxpr/psum | solution.py:80
  1539.5 28.8 %all_gather.17 = bf16[96,2048]{1,0:T(8,128)(2,1)S(1)} all-gather(bf16[96,256]{1,0:T(8,128)(2,1)S(1)} %fusion.96), channel_id=1, replica_groups=mesh['blk'=32,'lag'=8] {'lag'}, dimensions={1}, use_global_device_ids=true | all-gather | bytes 442368 | tf_op jit(solution)/shard_map/while/body/eval_jaxpr/all_gather | solution.py:84
  1580.7 36.8 %reduce-scatter.5.cloned.1.call-done = f32[256,96]{0,1:T(8,128)} async-done(((f32[2048,96]{0,1:T(8,128)}), f32[256,96]{0,1:T(8,128)}) %reduce-scatter.5.cloned.1.call-update) | async-done | bytes 98320 | tf_op jit(solution)/shard_map/while/body/eval_jaxpr/reduce_scatter | solution.py:50
  1618.5 17.5 %psum.25 = f32[96]{0:T(128)S(1)} all-reduce(f32[96]{0:T(128)S(1)} %broadcast_multiply_fusion.3), channel_id=1, replica_groups=mesh['blk'=32,'lag'=8] {'lag'}, use_global_device_ids=true, to_apply=%region_11.11 | all-reduce | flops 96 | bytes 768 | tf_op jit(solution)/shard_map/while/body/eval_jaxpr/psum | solution.py:80
  1637.0 28.9 %all_gather.17 = bf16[96,2048]{1,0:T(8,128)(2,1)S(1)} all-gather(bf16[96,256]{1,0:T(8,128)(2,1)S(1)} %fusion.96), channel_id=1, replica_groups=mesh['blk'=32,'lag'=8] {'lag'}, dimensions={1}, use_global_device_ids=true | all-gather | bytes 442368 | tf_op jit(solution)/shard_map/while/body/eval_jaxpr/all_gather | solution.py:84
  1669.6 7.4 collective-permute-done.2
  (524 shorter events, 170.8 us)
Async XLA Ops:
  6.5 52.4 %reduce-scatter.3.cloned.1.call-start = ((), (), s32[]{:S(2)}) async-start(), calls=%async_computation.2 | async-start | bytes 884736 | tf_op jit(solution)/shard_map/reduce_scatter | solution.py:50
  13.3 1.3 copy-start
  109.0 47.3 %reduce-scatter.5.cloned.1.call-start = ((), (), s32[]{:S(2)}) async-start(), calls=%async_computation.3 | async-start | bytes 884736 | tf_op jit(solution)/shard_map/while/body/eval_jaxpr/reduce_scatter | solution.py:50
  109.1 8.8 collective-permute-start
  119.4 86.7 %collective-permute-start.1 = (f32[128,768]{1,0:T(8,128)S(1)}, f32[128,768]{1,0:T(8,128)S(1)}, u32[]{:S(2)}, u32[]{:S(2)}) collective-permute-start(f32[128,768]{1,0:T(8,128)S(1)} %get-tuple-element.476), channel_id=1, source_target_pairs={{248,0},{0,8},{8,16},{16,24},{24,32},{32,40},{40,48},{48,56},{56,6... | collective-permute-start | bytes 1179656 | tf_op jit(solution)/shard_map/while/body/eval_jaxpr/ppermute | solution.py:11
  206.5 47.3 %reduce-scatter.5.cloned.1.call-start = ((), (), s32[]{:S(2)}) async-start(), calls=%async_computation.3 | async-start | bytes 884736 | tf_op jit(solution)/shard_map/while/body/eval_jaxpr/reduce_scatter | solution.py:50
  206.5 8.8 collective-permute-start
  216.9 86.5 %collective-permute-start.1 = (f32[128,768]{1,0:T(8,128)S(1)}, f32[128,768]{1,0:T(8,128)S(1)}, u32[]{:S(2)}, u32[]{:S(2)}) collective-permute-start(f32[128,768]{1,0:T(8,128)S(1)} %get-tuple-element.476), channel_id=1, source_target_pairs={{248,0},{0,8},{8,16},{16,24},{24,32},{32,40},{40,48},{48,56},{56,6... | collective-permute-start | bytes 1179656 | tf_op jit(solution)/shard_map/while/body/eval_jaxpr/ppermute | solution.py:11
  303.8 47.4 %reduce-scatter.5.cloned.1.call-start = ((), (), s32[]{:S(2)}) async-start(), calls=%async_computation.3 | async-start | bytes 884736 | tf_op jit(solution)/shard_map/while/body/eval_jaxpr/reduce_scatter | solution.py:50
  303.9 8.8 collective-permute-start
  314.3 86.7 %collective-permute-start.1 = (f32[128,768]{1,0:T(8,128)S(1)}, f32[128,768]{1,0:T(8,128)S(1)}, u32[]{:S(2)}, u32[]{:S(2)}) collective-permute-start(f32[128,768]{1,0:T(8,128)S(1)} %get-tuple-element.476), channel_id=1, source_target_pairs={{248,0},{0,8},{8,16},{16,24},{24,32},{32,40},{40,48},{48,56},{56,6... | collective-permute-start | bytes 1179656 | tf_op jit(solution)/shard_map/while/body/eval_jaxpr/ppermute | solution.py:11
  401.4 47.2 %reduce-scatter.5.cloned.1.call-start = ((), (), s32[]{:S(2)}) async-start(), calls=%async_computation.3 | async-start | bytes 884736 | tf_op jit(solution)/shard_map/while/body/eval_jaxpr/reduce_scatter | solution.py:50
  401.4 8.8 collective-permute-start
  411.8 86.5 %collective-permute-start.1 = (f32[128,768]{1,0:T(8,128)S(1)}, f32[128,768]{1,0:T(8,128)S(1)}, u32[]{:S(2)}, u32[]{:S(2)}) collective-permute-start(f32[128,768]{1,0:T(8,128)S(1)} %get-tuple-element.476), channel_id=1, source_target_pairs={{248,0},{0,8},{8,16},{16,24},{24,32},{32,40},{40,48},{48,56},{56,6... | collective-permute-start | bytes 1179656 | tf_op jit(solution)/shard_map/while/body/eval_jaxpr/ppermute | solution.py:11
  498.7 47.4 %reduce-scatter.5.cloned.1.call-start = ((), (), s32[]{:S(2)}) async-start(), calls=%async_computation.3 | async-start | bytes 884736 | tf_op jit(solution)/shard_map/while/body/eval_jaxpr/reduce_scatter | solution.py:50
  498.7 8.8 collective-permute-start
  509.1 86.6 %collective-permute-start.1 = (f32[128,768]{1,0:T(8,128)S(1)}, f32[128,768]{1,0:T(8,128)S(1)}, u32[]{:S(2)}, u32[]{:S(2)}) collective-permute-start(f32[128,768]{1,0:T(8,128)S(1)} %get-tuple-element.476), channel_id=1, source_target_pairs={{248,0},{0,8},{8,16},{16,24},{24,32},{32,40},{40,48},{48,56},{56,6... | collective-permute-start | bytes 1179656 | tf_op jit(solution)/shard_map/while/body/eval_jaxpr/ppermute | solution.py:11
  596.1 47.3 %reduce-scatter.5.cloned.1.call-start = ((), (), s32[]{:S(2)}) async-start(), calls=%async_computation.3 | async-start | bytes 884736 | tf_op jit(solution)/shard_map/while/body/eval_jaxpr/reduce_scatter | solution.py:50
  596.1 8.8 collective-permute-start
  606.5 86.6 %collective-permute-start.1 = (f32[128,768]{1,0:T(8,128)S(1)}, f32[128,768]{1,0:T(8,128)S(1)}, u32[]{:S(2)}, u32[]{:S(2)}) collective-permute-start(f32[128,768]{1,0:T(8,128)S(1)} %get-tuple-element.476), channel_id=1, source_target_pairs={{248,0},{0,8},{8,16},{16,24},{24,32},{32,40},{40,48},{48,56},{56,6... | collective-permute-start | bytes 1179656 | tf_op jit(solution)/shard_map/while/body/eval_jaxpr/ppermute | solution.py:11
  693.5 47.3 %reduce-scatter.5.cloned.1.call-start = ((), (), s32[]{:S(2)}) async-start(), calls=%async_computation.3 | async-start | bytes 884736 | tf_op jit(solution)/shard_map/while/body/eval_jaxpr/reduce_scatter | solution.py:50
  693.6 8.8 collective-permute-start
  704.0 86.6 %collective-permute-start.1 = (f32[128,768]{1,0:T(8,128)S(1)}, f32[128,768]{1,0:T(8,128)S(1)}, u32[]{:S(2)}, u32[]{:S(2)}) collective-permute-start(f32[128,768]{1,0:T(8,128)S(1)} %get-tuple-element.476), channel_id=1, source_target_pairs={{248,0},{0,8},{8,16},{16,24},{24,32},{32,40},{40,48},{48,56},{56,6... | collective-permute-start | bytes 1179656 | tf_op jit(solution)/shard_map/while/body/eval_jaxpr/ppermute | solution.py:11
  790.9 47.3 %reduce-scatter.5.cloned.1.call-start = ((), (), s32[]{:S(2)}) async-start(), calls=%async_computation.3 | async-start | bytes 884736 | tf_op jit(solution)/shard_map/while/body/eval_jaxpr/reduce_scatter | solution.py:50
  791.0 8.8 collective-permute-start
  801.4 86.6 %collective-permute-start.1 = (f32[128,768]{1,0:T(8,128)S(1)}, f32[128,768]{1,0:T(8,128)S(1)}, u32[]{:S(2)}, u32[]{:S(2)}) collective-permute-start(f32[128,768]{1,0:T(8,128)S(1)} %get-tuple-element.476), channel_id=1, source_target_pairs={{248,0},{0,8},{8,16},{16,24},{24,32},{32,40},{40,48},{48,56},{56,6... | collective-permute-start | bytes 1179656 | tf_op jit(solution)/shard_map/while/body/eval_jaxpr/ppermute | solution.py:11
  888.4 47.2 %reduce-scatter.5.cloned.1.call-start = ((), (), s32[]{:S(2)}) async-start(), calls=%async_computation.3 | async-start | bytes 884736 | tf_op jit(solution)/shard_map/while/body/eval_jaxpr/reduce_scatter | solution.py:50
  888.4 8.8 collective-permute-start
  898.8 86.5 %collective-permute-start.1 = (f32[128,768]{1,0:T(8,128)S(1)}, f32[128,768]{1,0:T(8,128)S(1)}, u32[]{:S(2)}, u32[]{:S(2)}) collective-permute-start(f32[128,768]{1,0:T(8,128)S(1)} %get-tuple-element.476), channel_id=1, source_target_pairs={{248,0},{0,8},{8,16},{16,24},{24,32},{32,40},{40,48},{48,56},{56,6... | collective-permute-start | bytes 1179656 | tf_op jit(solution)/shard_map/while/body/eval_jaxpr/ppermute | solution.py:11
  985.7 47.3 %reduce-scatter.5.cloned.1.call-start = ((), (), s32[]{:S(2)}) async-start(), calls=%async_computation.3 | async-start | bytes 884736 | tf_op jit(solution)/shard_map/while/body/eval_jaxpr/reduce_scatter | solution.py:50
  985.8 8.8 collective-permute-start
  996.1 86.6 %collective-permute-start.1 = (f32[128,768]{1,0:T(8,128)S(1)}, f32[128,768]{1,0:T(8,128)S(1)}, u32[]{:S(2)}, u32[]{:S(2)}) collective-permute-start(f32[128,768]{1,0:T(8,128)S(1)} %get-tuple-element.476), channel_id=1, source_target_pairs={{248,0},{0,8},{8,16},{16,24},{24,32},{32,40},{40,48},{48,56},{56,6... | collective-permute-start | bytes 1179656 | tf_op jit(solution)/shard_map/while/body/eval_jaxpr/ppermute | solution.py:11
  1083.1 47.3 %reduce-scatter.5.cloned.1.call-start = ((), (), s32[]{:S(2)}) async-start(), calls=%async_computation.3 | async-start | bytes 884736 | tf_op jit(solution)/shard_map/while/body/eval_jaxpr/reduce_scatter | solution.py:50
  1083.1 8.8 collective-permute-start
  1093.5 86.6 %collective-permute-start.1 = (f32[128,768]{1,0:T(8,128)S(1)}, f32[128,768]{1,0:T(8,128)S(1)}, u32[]{:S(2)}, u32[]{:S(2)}) collective-permute-start(f32[128,768]{1,0:T(8,128)S(1)} %get-tuple-element.476), channel_id=1, source_target_pairs={{248,0},{0,8},{8,16},{16,24},{24,32},{32,40},{40,48},{48,56},{56,6... | collective-permute-start | bytes 1179656 | tf_op jit(solution)/shard_map/while/body/eval_jaxpr/ppermute | solution.py:11
  1180.5 47.3 %reduce-scatter.5.cloned.1.call-start = ((), (), s32[]{:S(2)}) async-start(), calls=%async_computation.3 | async-start | bytes 884736 | tf_op jit(solution)/shard_map/while/body/eval_jaxpr/reduce_scatter | solution.py:50
  1180.6 8.8 collective-permute-start
  1191.0 86.6 %collective-permute-start.1 = (f32[128,768]{1,0:T(8,128)S(1)}, f32[128,768]{1,0:T(8,128)S(1)}, u32[]{:S(2)}, u32[]{:S(2)}) collective-permute-start(f32[128,768]{1,0:T(8,128)S(1)} %get-tuple-element.476), channel_id=1, source_target_pairs={{248,0},{0,8},{8,16},{16,24},{24,32},{32,40},{40,48},{48,56},{56,6... | collective-permute-start | bytes 1179656 | tf_op jit(solution)/shard_map/while/body/eval_jaxpr/ppermute | solution.py:11
  1277.9 47.3 %reduce-scatter.5.cloned.1.call-start = ((), (), s32[]{:S(2)}) async-start(), calls=%async_computation.3 | async-start | bytes 884736 | tf_op jit(solution)/shard_map/while/body/eval_jaxpr/reduce_scatter | solution.py:50
  1278.0 8.8 collective-permute-start
  1288.3 86.6 %collective-permute-start.1 = (f32[128,768]{1,0:T(8,128)S(1)}, f32[128,768]{1,0:T(8,128)S(1)}, u32[]{:S(2)}, u32[]{:S(2)}) collective-permute-start(f32[128,768]{1,0:T(8,128)S(1)} %get-tuple-element.476), channel_id=1, source_target_pairs={{248,0},{0,8},{8,16},{16,24},{24,32},{32,40},{40,48},{48,56},{56,6... | collective-permute-start | bytes 1179656 | tf_op jit(solution)/shard_map/while/body/eval_jaxpr/ppermute | solution.py:11
  1375.3 47.3 %reduce-scatter.5.cloned.1.call-start = ((), (), s32[]{:S(2)}) async-start(), calls=%async_computation.3 | async-start | bytes 884736 | tf_op jit(solution)/shard_map/while/body/eval_jaxpr/reduce_scatter | solution.py:50
  1375.4 8.8 collective-permute-start
  1385.8 86.6 %collective-permute-start.1 = (f32[128,768]{1,0:T(8,128)S(1)}, f32[128,768]{1,0:T(8,128)S(1)}, u32[]{:S(2)}, u32[]{:S(2)}) collective-permute-start(f32[128,768]{1,0:T(8,128)S(1)} %get-tuple-element.476), channel_id=1, source_target_pairs={{248,0},{0,8},{8,16},{16,24},{24,32},{32,40},{40,48},{48,56},{56,6... | collective-permute-start | bytes 1179656 | tf_op jit(solution)/shard_map/while/body/eval_jaxpr/ppermute | solution.py:11
  1472.8 47.2 %reduce-scatter.5.cloned.1.call-start = ((), (), s32[]{:S(2)}) async-start(), calls=%async_computation.3 | async-start | bytes 884736 | tf_op jit(solution)/shard_map/while/body/eval_jaxpr/reduce_scatter | solution.py:50
  1472.8 8.8 collective-permute-start
  1483.2 86.5 %collective-permute-start.1 = (f32[128,768]{1,0:T(8,128)S(1)}, f32[128,768]{1,0:T(8,128)S(1)}, u32[]{:S(2)}, u32[]{:S(2)}) collective-permute-start(f32[128,768]{1,0:T(8,128)S(1)} %get-tuple-element.476), channel_id=1, source_target_pairs={{248,0},{0,8},{8,16},{16,24},{24,32},{32,40},{40,48},{48,56},{56,6... | collective-permute-start | bytes 1179656 | tf_op jit(solution)/shard_map/while/body/eval_jaxpr/ppermute | solution.py:11
  1570.1 47.3 %reduce-scatter.5.cloned.1.call-start = ((), (), s32[]{:S(2)}) async-start(), calls=%async_computation.3 | async-start | bytes 884736 | tf_op jit(solution)/shard_map/while/body/eval_jaxpr/reduce_scatter | solution.py:50
  1570.2 8.8 collective-permute-start
  1580.5 86.7 %collective-permute-start.1 = (f32[128,768]{1,0:T(8,128)S(1)}, f32[128,768]{1,0:T(8,128)S(1)}, u32[]{:S(2)}, u32[]{:S(2)}) collective-permute-start(f32[128,768]{1,0:T(8,128)S(1)} %get-tuple-element.476), channel_id=1, source_target_pairs={{248,0},{0,8},{8,16},{16,24},{24,32},{32,40},{40,48},{48,56},{56,6... | collective-permute-start | bytes 1179656 | tf_op jit(solution)/shard_map/while/body/eval_jaxpr/ppermute | solution.py:11
  1667.6 9.4 collective-permute-start.2
Sparse Core Ops, SparseCore 0:
  16.2 42.7 reduce-scatter.2
  119.6 36.7 reduce-scatter.4
  217.0 36.6 reduce-scatter.4
  314.4 36.7 reduce-scatter.4
  411.9 36.5 reduce-scatter.4
  509.2 36.7 reduce-scatter.4
  606.6 36.7 reduce-scatter.4
  704.1 36.6 reduce-scatter.4
  801.5 36.7 reduce-scatter.4
  898.9 36.6 reduce-scatter.4
  996.3 36.6 reduce-scatter.4
  1093.6 36.7 reduce-scatter.4
  1191.1 36.6 reduce-scatter.4
  1288.5 36.7 reduce-scatter.4
  1385.9 36.6 reduce-scatter.4
  1483.3 36.6 reduce-scatter.4
  1580.7 36.7 reduce-scatter.4
where the time goes:
time: 1690 us; the launch traced here: 1680 us
  blocking collectives  788 us (47%)
  waiting for transfers between devices  743 us (44%)
  other arithmetic  53.9 us (3%)
  matrix products  48.1 us (3%)
  local copies, waits for them, and re-layouts  30.6 us (2%)
    reduce_scatter x17, waiting for transfers between devices, forward(): lax.psum_scatter(jnp.einsum('prf,rft->tp', cross, local_table, preferred_...  630 us
    all_gather x17, blocking collectives, correlate(): spectral = back(lax.all_gather(adjoint, 'lag', axis=1, tiled=True))  490 us
    psum x17, blocking collectives, correlate(): lax.psum(jnp.sum(weight[None, :] * lagged * lagged, axis=1) / lag_total,...  298 us
    ppermute x33, waiting for transfers between devices, from_behind(): return lax.ppermute(block, axis, route)  112 us
  transfers between devices with their start and end apart: 50, of which 34 were waited for; matrix products, arithmetic and copies ran while one was open for 5% of the time, Pallas kernels for 0%

commit v1 on v0

--- a/solution.py
+++ b/solution.py
@@ -81,7 +81,16 @@
         adjoint = (weight[None, :] * lagged / jnp.sqrt(energy + 1e-05)[:, None]).astype(
             jnp.bfloat16
         )
-        spectral = back(lax.all_gather(adjoint, "lag", axis=1, tiled=True))
+        begin_classes = lambda t0: jnp.concatenate(
+            jax.lax.all_to_all(
+                jnp.stack([t0 for _ in range(jax.lax.axis_size("lag"))]),
+                split_axis=0,
+                concat_axis=0,
+                axis_name="lag",
+            ),
+            1,
+        )
+        spectral = back(begin_classes(adjoint))
         adj_real = spectral[:, None, 0]
         adj_imag = spectral[:, None, 1]
         near = jnp.stack(

time: 1690 us -> 1450 us (0.86)
  blocking collectives: 788 us -> 297 us
  waiting for transfers between devices: 743 us -> 878 us
  starting transfers between devices: 5.33 us -> 73.5 us
  local copies, waits for them, and re-layouts: 30.6 us -> 64.6 us
    all_gather x17 -> x0, blocking collectives: 490 us -> none  [correlate(): spectral = back(lax.all_gather(adjoint, 'lag', axis=1, tiled=True))]
    all_to_all x0 -> x17, waiting for transfers between devices: none -> 105 us  [correlate(): jax.lax.all_to_all(jnp.stack([t0 for _ in range(jax.lax.axis_size('lag'))...]
    all_to_all x0 -> x17, starting transfers between devices: none -> 71.6 us  [correlate(): jax.lax.all_to_all(jnp.stack([t0 for _ in range(jax.lax.axis_size('lag'))...]
    ppermute x33, waiting for transfers between devices: 112 us -> 165 us  [from_behind(): return lax.ppermute(block, axis, route)]
    reduce_scatter x17, waiting for transfers between devices: 630 us -> 608 us  [forward(): lax.psum_scatter(jnp.einsum('prf,rft->tp', cross, local_table, preferred_...]
  transfers between devices with their start and end apart: 50 -> 67, of which waited for: 34 -> 67; matrix products, arithmetic and copies ran while one was open for 5% -> 5% of each run, Pallas kernels for 0% -> 0%
where the time goes in v1:
time: 1450 us; the launch traced here: 1440 us
  waiting for transfers between devices  878 us (61%)
  blocking collectives  297 us (20%)
  starting transfers between devices  73.5 us (5%)
  local copies, waits for them, and re-layouts  64.6 us (4%)
  matrix products  60.3 us (4%)
  other arithmetic  54.4 us (4%)
    reduce_scatter x17, waiting for transfers between devices, forward(): lax.psum_scatter(jnp.einsum('prf,rft->tp', cross, local_table, preferred_...  608 us
    psum x17, blocking collectives, correlate(): lax.psum(jnp.sum(weight[None, :] * lagged * lagged, axis=1) / lag_total,...  297 us
    ppermute x33, waiting for transfers between devices, from_behind(): return lax.ppermute(block, axis, route)  165 us
    all_to_all x17, waiting for transfers between devices, correlate(): jax.lax.all_to_all(jnp.stack([t0 for _ in range(jax.lax.axis_size('lag'))...  105 us
    all_to_all x17, starting transfers between devices, correlate(): jax.lax.all_to_all(jnp.stack([t0 for _ in range(jax.lax.axis_size('lag'))...  71.6 us
  transfers between devices with their start and end apart: 67, of which 67 were waited for; matrix products, arithmetic and copies ran while one was open for 5% of the time, Pallas kernels for 0%

profile of v1, /device:TPU:8, one launch (start us, length us, event | category | flops | bytes accessed | tf_op | source)
XLA Modules:
  0.0 1443.8 jit_solution(8710925715459551032)
XLA Ops:
  16.1 42.9 %reduce-scatter.3.cloned.1.call-done = f32[256,96]{0,1:T(8,128)} async-done(((f32[2048,96]{0,1:T(8,128)}), f32[256,96]{0,1:T(8,128)}) %reduce-scatter.3.cloned.1.call-update) | async-done | bytes 98320 | tf_op jit(solution)/shard_map/reduce_scatter | solution.py:50
  60.0 17.5 %psum.21 = f32[96]{0:T(128)S(1)} all-reduce(f32[96]{0:T(128)S(1)} %broadcast_multiply_fusion.1), channel_id=1, replica_groups=mesh['blk'=32,'lag'=8] {'lag'}, use_global_device_ids=true, to_apply=%region_5.6 | all-reduce | flops 96 | bytes 768 | tf_op jit(solution)/shard_map/psum | solution.py:80
  94.6 1332.3 %while.21 = (s32[]{:T(128)}, bf16[128,3,2,128]{0,3,2,1:T(8,128)(2,1)S(1)}, f32[128,768]{1,0:T(8,128)S(1)}, f32[128,768]{1,0:T(8,128)}, s32[1,17,96,2]{2,3,1,0:T(...) while((s32[]{:T(128)}, ...), condition=%wide.region_12.13_spmd.clone.clone, body=%wide.region_6.12_spmd.clone.clone.sunk | while | flops 278300032 | bytes 19705452 | solution.py:126
  97.0 6.4 collective-permute-done
  105.0 37.5 %reduce-scatter.5.cloned.1.call-done = f32[256,96]{0,1:T(8,128)} async-done(((f32[2048,96]{0,1:T(8,128)}), f32[256,96]{0,1:T(8,128)}) %reduce-scatter.5.cloned.1.call-update) | async-done | bytes 98320 | tf_op jit(solution)/shard_map/while/body/eval_jaxpr/reduce_scatter | solution.py:50
  143.5 17.5 %psum.25 = f32[96]{0:T(128)S(1)} all-reduce(f32[96]{0:T(128)S(1)} %broadcast_multiply_fusion.3), channel_id=1, replica_groups=mesh['blk'=32,'lag'=8] {'lag'}, use_global_device_ids=true, to_apply=%region_11.11 | all-reduce | flops 96 | bytes 768 | tf_op jit(solution)/shard_map/while/body/eval_jaxpr/psum | solution.py:80
  167.7 6.2 all-to-all-done
  182.4 6.4 collective-permute-done
  190.5 35.1 %reduce-scatter.5.cloned.1.call-done = f32[256,96]{0,1:T(8,128)} async-done(((f32[2048,96]{0,1:T(8,128)}), f32[256,96]{0,1:T(8,128)}) %reduce-scatter.5.cloned.1.call-update) | async-done | bytes 98320 | tf_op jit(solution)/shard_map/while/body/eval_jaxpr/reduce_scatter | solution.py:50
  226.6 17.5 %psum.25 = f32[96]{0:T(128)S(1)} all-reduce(f32[96]{0:T(128)S(1)} %broadcast_multiply_fusion.3), channel_id=1, replica_groups=mesh['blk'=32,'lag'=8] {'lag'}, use_global_device_ids=true, to_apply=%region_11.11 | all-reduce | flops 96 | bytes 768 | tf_op jit(solution)/shard_map/while/body/eval_jaxpr/psum | solution.py:80
  250.7 6.2 all-to-all-done
  265.5 6.4 collective-permute-done
  273.5 35.2 %reduce-scatter.5.cloned.1.call-done = f32[256,96]{0,1:T(8,128)} async-done(((f32[2048,96]{0,1:T(8,128)}), f32[256,96]{0,1:T(8,128)}) %reduce-scatter.5.cloned.1.call-update) | async-done | bytes 98320 | tf_op jit(solution)/shard_map/while/body/eval_jaxpr/reduce_scatter | solution.py:50
  309.7 17.5 %psum.25 = f32[96]{0:T(128)S(1)} all-reduce(f32[96]{0:T(128)S(1)} %broadcast_multiply_fusion.3), channel_id=1, replica_groups=mesh['blk'=32,'lag'=8] {'lag'}, use_global_device_ids=true, to_apply=%region_11.11 | all-reduce | flops 96 | bytes 768 | tf_op jit(solution)/shard_map/while/body/eval_jaxpr/psum | solution.py:80
  348.7 6.4 collective-permute-done
  356.7 35.1 %reduce-scatter.5.cloned.1.call-done = f32[256,96]{0,1:T(8,128)} async-done(((f32[2048,96]{0,1:T(8,128)}), f32[256,96]{0,1:T(8,128)}) %reduce-scatter.5.cloned.1.call-update) | async-done | bytes 98320 | tf_op jit(solution)/shard_map/while/body/eval_jaxpr/reduce_scatter | solution.py:50
  392.8 17.5 %psum.25 = f32[96]{0:T(128)S(1)} all-reduce(f32[96]{0:T(128)S(1)} %broadcast_multiply_fusion.3), channel_id=1, replica_groups=mesh['blk'=32,'lag'=8] {'lag'}, use_global_device_ids=true, to_apply=%region_11.11 | all-reduce | flops 96 | bytes 768 | tf_op jit(solution)/shard_map/while/body/eval_jaxpr/psum | solution.py:80
  417.1 6.3 all-to-all-done
  431.8 6.4 collective-permute-done
  439.9 35.1 %reduce-scatter.5.cloned.1.call-done = f32[256,96]{0,1:T(8,128)} async-done(((f32[2048,96]{0,1:T(8,128)}), f32[256,96]{0,1:T(8,128)}) %reduce-scatter.5.cloned.1.call-update) | async-done | bytes 98320 | tf_op jit(solution)/shard_map/while/body/eval_jaxpr/reduce_scatter | solution.py:50
  475.9 17.5 %psum.25 = f32[96]{0:T(128)S(1)} all-reduce(f32[96]{0:T(128)S(1)} %broadcast_multiply_fusion.3), channel_id=1, replica_groups=mesh['blk'=32,'lag'=8] {'lag'}, use_global_device_ids=true, to_apply=%region_11.11 | all-reduce | flops 96 | bytes 768 | tf_op jit(solution)/shard_map/while/body/eval_jaxpr/psum | solution.py:80
  500.1 6.2 all-to-all-done
  514.9 6.4 collective-permute-done
  522.9 35.2 %reduce-scatter.5.cloned.1.call-done = f32[256,96]{0,1:T(8,128)} async-done(((f32[2048,96]{0,1:T(8,128)}), f32[256,96]{0,1:T(8,128)}) %reduce-scatter.5.cloned.1.call-update) | async-done | bytes 98320 | tf_op jit(solution)/shard_map/while/body/eval_jaxpr/reduce_scatter | solution.py:50
  559.1 17.4 %psum.25 = f32[96]{0:T(128)S(1)} all-reduce(f32[96]{0:T(128)S(1)} %broadcast_multiply_fusion.3), channel_id=1, replica_groups=mesh['blk'=32,'lag'=8] {'lag'}, use_global_device_ids=true, to_apply=%region_11.11 | all-reduce | flops 96 | bytes 768 | tf_op jit(solution)/shard_map/while/body/eval_jaxpr/psum | solution.py:80
  583.2 6.2 all-to-all-done
  598.0 6.4 collective-permute-done
  606.0 35.2 %reduce-scatter.5.cloned.1.call-done = f32[256,96]{0,1:T(8,128)} async-done(((f32[2048,96]{0,1:T(8,128)}), f32[256,96]{0,1:T(8,128)}) %reduce-scatter.5.cloned.1.call-update) | async-done | bytes 98320 | tf_op jit(solution)/shard_map/while/body/eval_jaxpr/reduce_scatter | solution.py:50
  642.2 17.4 %psum.25 = f32[96]{0:T(128)S(1)} all-reduce(f32[96]{0:T(128)S(1)} %broadcast_multiply_fusion.3), channel_id=1, replica_groups=mesh['blk'=32,'lag'=8] {'lag'}, use_global_device_ids=true, to_apply=%region_11.11 | all-reduce | flops 96 | bytes 768 | tf_op jit(solution)/shard_map/while/body/eval_jaxpr/psum | solution.py:80
  666.3 6.2 all-to-all-done
  681.1 6.4 collective-permute-done
  689.1 35.2 %reduce-scatter.5.cloned.1.call-done = f32[256,96]{0,1:T(8,128)} async-done(((f32[2048,96]{0,1:T(8,128)}), f32[256,96]{0,1:T(8,128)}) %reduce-scatter.5.cloned.1.call-update) | async-done | bytes 98320 | tf_op jit(solution)/shard_map/while/body/eval_jaxpr/reduce_scatter | solution.py:50
  725.3 17.5 %psum.25 = f32[96]{0:T(128)S(1)} all-reduce(f32[96]{0:T(128)S(1)} %broadcast_multiply_fusion.3), channel_id=1, replica_groups=mesh['blk'=32,'lag'=8] {'lag'}, use_global_device_ids=true, to_apply=%region_11.11 | all-reduce | flops 96 | bytes 768 | tf_op jit(solution)/shard_map/while/body/eval_jaxpr/psum | solution.py:80
  749.5 6.2 all-to-all-done
  764.3 6.4 collective-permute-done
  772.3 35.2 %reduce-scatter.5.cloned.1.call-done = f32[256,96]{0,1:T(8,128)} async-done(((f32[2048,96]{0,1:T(8,128)}), f32[256,96]{0,1:T(8,128)}) %reduce-scatter.5.cloned.1.call-update) | async-done | bytes 98320 | tf_op jit(solution)/shard_map/while/body/eval_jaxpr/reduce_scatter | solution.py:50
  808.5 17.4 %psum.25 = f32[96]{0:T(128)S(1)} all-reduce(f32[96]{0:T(128)S(1)} %broadcast_multiply_fusion.3), channel_id=1, replica_groups=mesh['blk'=32,'lag'=8] {'lag'}, use_global_device_ids=true, to_apply=%region_11.11 | all-reduce | flops 96 | bytes 768 | tf_op jit(solution)/shard_map/while/body/eval_jaxpr/psum | solution.py:80
  832.6 6.2 all-to-all-done
  847.3 6.4 collective-permute-done
  855.4 35.2 %reduce-scatter.5.cloned.1.call-done = f32[256,96]{0,1:T(8,128)} async-done(((f32[2048,96]{0,1:T(8,128)}), f32[256,96]{0,1:T(8,128)}) %reduce-scatter.5.cloned.1.call-update) | async-done | bytes 98320 | tf_op jit(solution)/shard_map/while/body/eval_jaxpr/reduce_scatter | solution.py:50
  891.6 17.4 %psum.25 = f32[96]{0:T(128)S(1)} all-reduce(f32[96]{0:T(128)S(1)} %broadcast_multiply_fusion.3), channel_id=1, replica_groups=mesh['blk'=32,'lag'=8] {'lag'}, use_global_device_ids=true, to_apply=%region_11.11 | all-reduce | flops 96 | bytes 768 | tf_op jit(solution)/shard_map/while/body/eval_jaxpr/psum | solution.py:80
  930.4 6.4 collective-permute-done
  938.4 35.2 %reduce-scatter.5.cloned.1.call-done = f32[256,96]{0,1:T(8,128)} async-done(((f32[2048,96]{0,1:T(8,128)}), f32[256,96]{0,1:T(8,128)}) %reduce-scatter.5.cloned.1.call-update) | async-done | bytes 98320 | tf_op jit(solution)/shard_map/while/body/eval_jaxpr/reduce_scatter | solution.py:50
  974.7 17.5 %psum.25 = f32[96]{0:T(128)S(1)} all-reduce(f32[96]{0:T(128)S(1)} %broadcast_multiply_fusion.3), channel_id=1, replica_groups=mesh['blk'=32,'lag'=8] {'lag'}, use_global_device_ids=true, to_apply=%region_11.11 | all-reduce | flops 96 | bytes 768 | tf_op jit(solution)/shard_map/while/body/eval_jaxpr/psum | solution.py:80
  998.8 6.2 all-to-all-done
  1013.6 6.4 collective-permute-done
  1021.6 35.2 %reduce-scatter.5.cloned.1.call-done = f32[256,96]{0,1:T(8,128)} async-done(((f32[2048,96]{0,1:T(8,128)}), f32[256,96]{0,1:T(8,128)}) %reduce-scatter.5.cloned.1.call-update) | async-done | bytes 98320 | tf_op jit(solution)/shard_map/while/body/eval_jaxpr/reduce_scatter | solution.py:50
  1057.8 17.4 %psum.25 = f32[96]{0:T(128)S(1)} all-reduce(f32[96]{0:T(128)S(1)} %broadcast_multiply_fusion.3), channel_id=1, replica_groups=mesh['blk'=32,'lag'=8] {'lag'}, use_global_device_ids=true, to_apply=%region_11.11 | all-reduce | flops 96 | bytes 768 | tf_op jit(solution)/shard_map/while/body/eval_jaxpr/psum | solution.py:80
  1096.6 6.4 collective-permute-done
  1104.6 35.2 %reduce-scatter.5.cloned.1.call-done = f32[256,96]{0,1:T(8,128)} async-done(((f32[2048,96]{0,1:T(8,128)}), f32[256,96]{0,1:T(8,128)}) %reduce-scatter.5.cloned.1.call-update) | async-done | bytes 98320 | tf_op jit(solution)/shard_map/while/body/eval_jaxpr/reduce_scatter | solution.py:50
  1140.9 17.5 %psum.25 = f32[96]{0:T(128)S(1)} all-reduce(f32[96]{0:T(128)S(1)} %broadcast_multiply_fusion.3), channel_id=1, replica_groups=mesh['blk'=32,'lag'=8] {'lag'}, use_global_device_ids=true, to_apply=%region_11.11 | all-reduce | flops 96 | bytes 768 | tf_op jit(solution)/shard_map/while/body/eval_jaxpr/psum | solution.py:80
  1179.7 6.4 collective-permute-done
  1187.7 35.2 %reduce-scatter.5.cloned.1.call-done = f32[256,96]{0,1:T(8,128)} async-done(((f32[2048,96]{0,1:T(8,128)}), f32[256,96]{0,1:T(8,128)}) %reduce-scatter.5.cloned.1.call-update) | async-done | bytes 98320 | tf_op jit(solution)/shard_map/while/body/eval_jaxpr/reduce_scatter | solution.py:50
  1224.0 17.4 %psum.25 = f32[96]{0:T(128)S(1)} all-reduce(f32[96]{0:T(128)S(1)} %broadcast_multiply_fusion.3), channel_id=1, replica_groups=mesh['blk'=32,'lag'=8] {'lag'}, use_global_device_ids=true, to_apply=%region_11.11 | all-reduce | flops 96 | bytes 768 | tf_op jit(solution)/shard_map/while/body/eval_jaxpr/psum | solution.py:80
  1248.1 6.2 all-to-all-done
  1262.9 6.4 collective-permute-done
  1270.9 35.2 %reduce-scatter.5.cloned.1.call-done = f32[256,96]{0,1:T(8,128)} async-done(((f32[2048,96]{0,1:T(8,128)}), f32[256,96]{0,1:T(8,128)}) %reduce-scatter.5.cloned.1.call-update) | async-done | bytes 98320 | tf_op jit(solution)/shard_map/while/body/eval_jaxpr/reduce_scatter | solution.py:50
  1307.1 17.5 %psum.25 = f32[96]{0:T(128)S(1)} all-reduce(f32[96]{0:T(128)S(1)} %broadcast_multiply_fusion.3), channel_id=1, replica_groups=mesh['blk'=32,'lag'=8] {'lag'}, use_global_device_ids=true, to_apply=%region_11.11 | all-reduce | flops 96 | bytes 768 | tf_op jit(solution)/shard_map/while/body/eval_jaxpr/psum | solution.py:80
  1331.2 6.2 all-to-all-done
  1346.0 6.4 collective-permute-done
  1354.0 35.2 %reduce-scatter.5.cloned.1.call-done = f32[256,96]{0,1:T(8,128)} async-done(((f32[2048,96]{0,1:T(8,128)}), f32[256,96]{0,1:T(8,128)}) %reduce-scatter.5.cloned.1.call-update) | async-done | bytes 98320 | tf_op jit(solution)/shard_map/while/body/eval_jaxpr/reduce_scatter | solution.py:50
  1390.2 17.5 %psum.25 = f32[96]{0:T(128)S(1)} all-reduce(f32[96]{0:T(128)S(1)} %broadcast_multiply_fusion.3), channel_id=1, replica_groups=mesh['blk'=32,'lag'=8] {'lag'}, use_global_device_ids=true, to_apply=%region_11.11 | all-reduce | flops 96 | bytes 768 | tf_op jit(solution)/shard_map/while/body/eval_jaxpr/psum | solution.py:80
  1414.3 6.2 all-to-all-done
  1428.4 7.9 collective-permute-done.2
  (626 shorter events, 338.0 us)
Async XLA Ops:
  6.5 52.4 %reduce-scatter.3.cloned.1.call-start = ((), (), s32[]{:S(2)}) async-start(), calls=%async_computation.4 | async-start | bytes 884736 | tf_op jit(solution)/shard_map/reduce_scatter | solution.py:50
  79.2 10.7 all-to-all-start.1
  94.6 47.9 %reduce-scatter.5.cloned.1.call-start = ((), (), s32[]{:S(2)}) async-start(), calls=%async_computation.5 | async-start | bytes 884736 | tf_op jit(solution)/shard_map/while/body/eval_jaxpr/reduce_scatter | solution.py:50
  94.6 8.8 collective-permute-start
  162.8 11.1 all-to-all-start
  167.0 12.1 collective-permute-start.1
  180.1 45.4 %reduce-scatter.5.cloned.1.call-start = ((), (), s32[]{:S(2)}) async-start(), calls=%async_computation.5 | async-start | bytes 884736 | tf_op jit(solution)/shard_map/while/body/eval_jaxpr/reduce_scatter | solution.py:50
  180.1 8.7 collective-permute-start
  245.8 11.0 all-to-all-start
  250.0 12.1 collective-permute-start.1
  263.2 45.5 %reduce-scatter.5.cloned.1.call-start = ((), (), s32[]{:S(2)}) async-start(), calls=%async_computation.5 | async-start | bytes 884736 | tf_op jit(solution)/shard_map/while/body/eval_jaxpr/reduce_scatter | solution.py:50
  263.2 8.7 collective-permute-start
  329.0 11.1 all-to-all-start
  333.2 12.1 collective-permute-start.1
  346.4 45.4 %reduce-scatter.5.cloned.1.call-start = ((), (), s32[]{:S(2)}) async-start(), calls=%async_computation.5 | async-start | bytes 884736 | tf_op jit(solution)/shard_map/while/body/eval_jaxpr/reduce_scatter | solution.py:50
  346.4 8.7 collective-permute-start
  412.1 11.3 all-to-all-start
  416.4 12.0 collective-permute-start.1
  429.5 45.4 %reduce-scatter.5.cloned.1.call-start = ((), (), s32[]{:S(2)}) async-start(), calls=%async_computation.5 | async-start | bytes 884736 | tf_op jit(solution)/shard_map/while/body/eval_jaxpr/reduce_scatter | solution.py:50
  429.5 8.7 collective-permute-start
  495.2 11.0 all-to-all-start
  499.4 12.1 collective-permute-start.1
  512.6 45.5 %reduce-scatter.5.cloned.1.call-start = ((), (), s32[]{:S(2)}) async-start(), calls=%async_computation.5 | async-start | bytes 884736 | tf_op jit(solution)/shard_map/while/body/eval_jaxpr/reduce_scatter | solution.py:50
  512.6 8.7 collective-permute-start
  578.3 11.1 all-to-all-start
  582.5 12.1 collective-permute-start.1
  595.7 45.5 %reduce-scatter.5.cloned.1.call-start = ((), (), s32[]{:S(2)}) async-start(), calls=%async_computation.5 | async-start | bytes 884736 | tf_op jit(solution)/shard_map/while/body/eval_jaxpr/reduce_scatter | solution.py:50
  595.7 8.7 collective-permute-start
  661.4 11.1 all-to-all-start
  665.6 12.1 collective-permute-start.1
  678.8 45.5 %reduce-scatter.5.cloned.1.call-start = ((), (), s32[]{:S(2)}) async-start(), calls=%async_computation.5 | async-start | bytes 884736 | tf_op jit(solution)/shard_map/while/body/eval_jaxpr/reduce_scatter | solution.py:50
  678.8 8.7 collective-permute-start
  744.6 11.1 all-to-all-start
  748.8 12.1 collective-permute-start.1
  762.0 45.5 %reduce-scatter.5.cloned.1.call-start = ((), (), s32[]{:S(2)}) async-start(), calls=%async_computation.5 | async-start | bytes 884736 | tf_op jit(solution)/shard_map/while/body/eval_jaxpr/reduce_scatter | solution.py:50
  762.0 8.7 collective-permute-start
  827.7 11.1 all-to-all-start
  831.9 12.1 collective-permute-start.1
  845.0 45.5 %reduce-scatter.5.cloned.1.call-start = ((), (), s32[]{:S(2)}) async-start(), calls=%async_computation.5 | async-start | bytes 884736 | tf_op jit(solution)/shard_map/while/body/eval_jaxpr/reduce_scatter | solution.py:50
  845.0 8.7 collective-permute-start
  910.8 11.0 all-to-all-start
  915.0 12.1 collective-permute-start.1
  928.1 45.5 %reduce-scatter.5.cloned.1.call-start = ((), (), s32[]{:S(2)}) async-start(), calls=%async_computation.5 | async-start | bytes 884736 | tf_op jit(solution)/shard_map/while/body/eval_jaxpr/reduce_scatter | solution.py:50
  928.1 8.7 collective-permute-start
  993.9 11.1 all-to-all-start
  998.1 12.1 collective-permute-start.1
  1011.3 45.5 %reduce-scatter.5.cloned.1.call-start = ((), (), s32[]{:S(2)}) async-start(), calls=%async_computation.5 | async-start | bytes 884736 | tf_op jit(solution)/shard_map/while/body/eval_jaxpr/reduce_scatter | solution.py:50
  1011.3 8.7 collective-permute-start
  1077.0 11.0 all-to-all-start
  1081.2 12.1 collective-permute-start.1
  1094.3 45.5 %reduce-scatter.5.cloned.1.call-start = ((), (), s32[]{:S(2)}) async-start(), calls=%async_computation.5 | async-start | bytes 884736 | tf_op jit(solution)/shard_map/while/body/eval_jaxpr/reduce_scatter | solution.py:50
  1160.2 10.9 all-to-all-start
  1164.3 12.1 collective-permute-start.1
  1177.4 45.5 %reduce-scatter.5.cloned.1.call-start = ((), (), s32[]{:S(2)}) async-start(), calls=%async_computation.5 | async-start | bytes 884736 | tf_op jit(solution)/shard_map/while/body/eval_jaxpr/reduce_scatter | solution.py:50
  1243.2 11.1 all-to-all-start
  1247.4 12.1 collective-permute-start.1
  1260.6 45.5 %reduce-scatter.5.cloned.1.call-start = ((), (), s32[]{:S(2)}) async-start(), calls=%async_computation.5 | async-start | bytes 884736 | tf_op jit(solution)/shard_map/while/body/eval_jaxpr/reduce_scatter | solution.py:50
  1326.3 11.1 all-to-all-start
  1330.5 12.1 collective-permute-start.1
  1343.7 45.5 %reduce-scatter.5.cloned.1.call-start = ((), (), s32[]{:S(2)}) async-start(), calls=%async_computation.5 | async-start | bytes 884736 | tf_op jit(solution)/shard_map/while/body/eval_jaxpr/reduce_scatter | solution.py:50
  1343.7 8.7 collective-permute-start
  1409.4 11.1 all-to-all-start
  1413.7 12.1 collective-permute-start.1
  1426.8 9.5 collective-permute-start.2
  (21 other events, 108.2 us)
Sparse Core Ops, SparseCore 0:
  16.2 42.7 reduce-scatter.2
  105.1 37.3 reduce-scatter.4
  190.6 34.9 reduce-scatter.4
  273.6 35.0 reduce-scatter.4
  356.8 34.9 reduce-scatter.4
  440.0 34.9 reduce-scatter.4
  523.0 35.0 reduce-scatter.4
  606.1 35.0 reduce-scatter.4
  689.2 35.0 reduce-scatter.4
  772.4 35.0 reduce-scatter.4
  855.5 35.0 reduce-scatter.4
  938.5 35.0 reduce-scatter.4
  1021.7 35.0 reduce-scatter.4
  1104.7 35.0 reduce-scatter.4
  1187.8 35.0 reduce-scatter.4
  1271.0 35.0 reduce-scatter.4
  1354.1 35.0 reduce-scatter.4
